TPU v7x, 32 devices: a whole 2x2x4 slice. The times are simulated.
32 devices in a mesh: mem: 8 (over z, core), tile: 4 (over y, x).
Axes of the slice: x: 2, y: 2, z: 4, core: 2. Of those that a mesh axis runs over, the one named last changes fastest.
Arguments:
- right_side: float32 [8, 32, 512], P(None, 'tile'), may hold values from -6 to 6
- members: bfloat16 [8, 8, 32, 512], P('mem', None, 'tile'), may hold values from -6 to 6
- diffusivity: float32 [8, 32, 512], P(None, 'tile'), may hold values from 0.02 to 0.12
- obs_index: int32 [8192], P('tile'), may hold values from 0 to 32767, as said below
- obs_precision: float32 [8192], P('tile'), may hold values from 0.5 to 4
Outputs:
- increment: float32 [8, 32, 512], P(None, 'tile')
- residual: float32 [8, 32, 512], P(None, 'tile')
Inputs may be any that keep to these rules, and one draw needn't show every extreme that they name: `obs_index`: each entry is a flat cell index (level, row within the tile, column; column fastest) inside the block of the tile that holds the observation; several observations may share a cell.
All inputs are finite; a program needn't handle non-finite values.
Results may differ from a plain program's by a relative error of at most 0.0003.
Values sent between devices are 32-bit elements; how exact they have to be, the bound alone decides.
A program may use at most 64 MiB of HBM per device.

v0:
```python
import jax
import jax.numpy as jnp
from jax import lax
from jax.sharding import PartitionSpec as P

SWEEPS = 8
ITERS = 2


def padded(shard, sides, width):
    for axis, dim in sides:
        size, length = (lax.axis_size(axis), shard.shape[dim])
        up = [(i, (i + 1) % size) for i in range(size - 1)]
        down = [(j, i) for i, j in up]
        last = lax.slice_in_dim(shard, length - width, length, axis=dim)
        leading = lax.slice_in_dim(shard, 0, width, axis=dim)
        before = lax.ppermute(last, axis, up)
        after = lax.ppermute(leading, axis, down)
        shard = jnp.concatenate([before, shard, after], axis=dim)
    return shard


def sweep(field, kappa):
    centre = field[:, 1:-1]
    middle = kappa[:, 1:-1]
    flux = 0.5 * (middle + kappa[:, 2:]) * (field[:, 2:] - centre)
    flux = flux + 0.5 * (middle + kappa[:, :-2]) * (field[:, :-2] - centre)
    fpad = jnp.pad(centre, ((0, 0), (0, 0), (1, 1)))
    kpad = jnp.pad(middle, ((0, 0), (0, 0), (1, 1)))
    flux = flux + 0.5 * (middle + kpad[:, :, 2:]) * (fpad[:, :, 2:] - centre)
    flux = flux + 0.5 * (middle + kpad[:, :, :-2]) * (fpad[:, :, :-2] - centre)
    return centre + flux


def local(right_side, members, diffusivity, obs_index, obs_precision):
    levels, rows, width = right_side.shape
    level = obs_index // (rows * width)
    row_pos = obs_index // width % rows
    column = obs_index % width
    weight = jnp.zeros(right_side.shape, jnp.float32).at[level, row_pos, column].add(obs_precision)
    tile_pos = lax.axis_index("tile")
    all_rows = rows * lax.axis_size("tile")
    total_members = members.shape[0] * lax.axis_size("mem")
    depth_rim = SWEEPS
    kappa_rim = padded(diffusivity, (("tile", 1),), depth_rim)

    def inner(first, second):
        return lax.psum(jnp.sum(first * second), "tile")

    increment = jnp.zeros_like(right_side)
    residual, direction = (right_side, right_side)
    norm_now = inner(residual, residual)
    for step in range(ITERS):
        pert = members[0].astype(jnp.float32)
        extended = padded(pert * direction, (("tile", 1),), SWEEPS)
        for localize_step in range(SWEEPS):
            depth = SWEEPS - localize_step - 1
            kappa = kappa_rim[:, localize_step : kappa_rim.shape[1] - localize_step]
            extended = sweep(extended, kappa)
            global_row = tile_pos * rows - depth + jnp.arange(rows + 2 * depth, dtype=jnp.int32)
            inside = (global_row >= 0) & (global_row < all_rows)
            extended = jnp.where(inside[None, :, None], extended, 0.0)
        total = pert * extended
        operate_total = lax.psum(total, "mem")
        image = direction + weight * direction + operate_total / total_members
        alpha = norm_now / inner(direction, image)
        increment = increment + alpha * direction
        residual = residual - alpha * image
        if step + 1 < ITERS:
            norm_next = inner(residual, residual)
            direction = residual + norm_next / norm_now * direction
            norm_now = norm_next
    return (increment, residual)


def solution(mesh):
    in_specs = (
        P(None, "tile", None),
        P("mem", None, "tile", None),
        P(None, "tile", None),
        P("tile"),
        P("tile"),
    )
    out_specs = (P(None, "tile", None), P(None, "tile", None))
    return jax.shard_map(local, mesh=mesh, in_specs=in_specs, out_specs=out_specs, check_vma=False)
```

profile of v0, /device:TPU:0, one launch (start us, length us, event | category | flops | bytes accessed | tf_op | source)
XLA Modules:
  0.0 210.4 jit_solution(3690111148064844957)
XLA Ops:
  7.2 1.0 convert_multiply_fusion.3
  8.2 1.3 collective-permute-start.1
  9.5 6.2 %collective-permute-start = (f32[8,8,512]{2,1,0:T(8,128)S(1)}, f32[8,8,512]{2,1,0:T(8,128)}, u32[]{:S(2)}, u32[]{:S(2)}) collective-permute-start(f32[8,8,512]{2,1,0:T(8,128)S(1)} %convert_multiply_fusion.3), channel_id=1, source_target_pairs={{0,1},{1,2},{2,3},{4,5},{5,6},{6,7},{8,9},{9,10},{10,11},{12,13},{... | collective-permute-start | bytes 393224 | tf_op jit(solution)/shard_map/ppermute | solution.py:17
  15.6 1.3 collective-permute-start.3
  16.9 4.8 %collective-permute-start.2 = (f32[8,8,512]{2,1,0:T(8,128)S(1)}, f32[8,8,512]{2,1,0:T(8,128)S(1)}, u32[]{:S(2)}, u32[]{:S(2)}) collective-permute-start(f32[8,8,512]{2,1,0:T(8,128)S(1)} %copy-done.1), channel_id=1, source_target_pairs={{0,1},{1,2},{2,3},{4,5},{5,6},{6,7},{8,9},{9,10},{10,11},{12,13},{... | collective-permute-start | bytes 393224 | tf_op jit(solution)/shard_map/ppermute | solution.py:17
  22.5 0.6 copy-done.21
  23.3 0.6 copy-done.22
  24.7 0.9 pad_maximum_fusion
  26.3 0.6 fusion.21
  29.4 0.8 copy-done.3
  30.2 0.9 convert_multiply_fusion.2
  31.1 11.5 %scatter_custom_fusion = f32[32768]{0:T(1024)S(1)} fusion(s32[2048]{0:T(1024)S(1)} %broadcast_select_fusion, f32[2048]{0:T(1024)} %param.9, f32[]{:T(128)} %constant.43.clone.1), kind=kCustom, calls=%fused_computation.339 | custom fusion | flops 2048 | bytes 131584
  42.6 47.1 %all-reduce.28.cloned.1.call-done = f32[8,8,512]{2,1,0:T(8,128)} async-done(((f32[8,8,512]{2,1,0:T(8,128)}), f32[8,8,512]{2,1,0:T(8,128)}) %all-reduce.28.cloned.1.call-update) | async-done | bytes 131088 | tf_op jit(solution)/shard_map/psum | solution.py:64
  89.7 1.6 multiply_reduce_fusion.2
  91.3 10.4 %all-reduce.24 = (f32[]{:T(128)}, f32[]{:T(128)}) all-reduce(f32[]{:T(128)} %get-tuple-element.3, f32[]{:T(128)} %get-tuple-element.2), channel_id=1, replica_groups=mesh['mem'=8,'tile'=4] {'tile'}, use_global_device_ids=true, to_apply=%region_1.2 | all-reduce | flops 2 | bytes 16 | tf_op jit(solution)/shard_map/psum | solution.py:48
  103.1 1.6 multiply_reduce_fusion.1
  104.6 8.7 %psum.45 = f32[]{:T(128)} all-reduce(f32[]{:T(128)} %get-tuple-element.6), channel_id=1, replica_groups=mesh['mem'=8,'tile'=4] {'tile'}, use_global_device_ids=true, to_apply=%region_7.8 | all-reduce | flops 1 | bytes 8 | tf_op jit(solution)/shard_map/psum | solution.py:48
  114.7 0.9 convert_multiply_fusion.1
  115.5 1.3 collective-permute-start.5
  116.8 4.6 %collective-permute-start.4 = (f32[8,8,512]{2,1,0:T(8,128)S(1)}, f32[8,8,512]{2,1,0:T(8,128)S(1)}, u32[]{:S(2)}, u32[]{:S(2)}) collective-permute-start(f32[8,8,512]{2,1,0:T(8,128)S(1)} %convert_multiply_fusion.1), channel_id=1, source_target_pairs={{0,1},{1,2},{2,3},{4,5},{5,6},{6,7},{8,9},{9,10},{10,11},{12,13},{... | collective-permute-start | bytes 393224 | tf_op jit(solution)/shard_map/ppermute | solution.py:17
  121.4 1.0 collective-permute-done.5
  122.4 1.5 collective-permute-done.4
  124.0 0.6 copy-done.12
  127.5 0.6 copy-done.20
  129.5 0.6 copy-done.16
  130.5 0.6 copy-done.14
  131.5 0.9 copy-done.2
  132.4 0.9 convert_multiply_fusion
  133.3 56.0 %all-reduce.30.cloned.1.call-done = f32[8,8,512]{2,1,0:T(8,128)} async-done(((f32[8,8,512]{2,1,0:T(8,128)}), f32[8,8,512]{2,1,0:T(8,128)}) %all-reduce.30.cloned.1.call-update) | async-done | bytes 131088 | tf_op jit(solution)/shard_map/psum | solution.py:64
  189.3 1.6 multiply_reduce_fusion
  190.9 10.4 %psum.47 = f32[]{:T(128)} all-reduce(f32[]{:T(128)} %multiply_reduce_fusion), channel_id=1, replica_groups=mesh['mem'=8,'tile'=4] {'tile'}, use_global_device_ids=true, to_apply=%region_10.11 | all-reduce | flops 1 | bytes 8 | tf_op jit(solution)/shard_map/psum | solution.py:48
  202.8 0.8 multiply_subtract_fusion
  (99 shorter events, 9.7 us)
Async XLA Ops:
  7.2 8.5 %copy-start.1 = (f32[8,8,512]{2,1,0:T(8,128)S(1)}, f32[8,8,512]{2,1,0:T(8,128)}, u32[]{:S(2)}) copy-start(f32[8,8,512]{2,1,0:T(8,128)} %param.7) | copy-start | bytes 393220
  7.2 82.5 %all-reduce.28.cloned.1.call-start = ((), (), s32[]{:S(2)}) async-start(), calls=%async_computation | async-start | bytes 262144 | tf_op jit(solution)/shard_map/psum | solution.py:64
  8.2 16.5 %collective-permute-start.1 = (f32[8,8,512]{2,1,0:T(8,128)S(1)}, f32[8,8,512]{2,1,0:T(8,128)S(1)}, u32[]{:S(2)}, u32[]{:S(2)}) collective-permute-start(f32[8,8,512]{2,1,0:T(8,128)S(1)} %convert_multiply_fusion.3), channel_id=1, source_target_pairs={{1,0},{2,1},{3,2},{5,4},{6,5},{7,6},{9,8},{10,9},{11,10},{13,12},{... | collective-permute-start | bytes 393224 | tf_op jit(solution)/shard_map/ppermute | solution.py:18
  9.5 15.2 %collective-permute-start = (f32[8,8,512]{2,1,0:T(8,128)S(1)}, f32[8,8,512]{2,1,0:T(8,128)}, u32[]{:S(2)}, u32[]{:S(2)}) collective-permute-start(f32[8,8,512]{2,1,0:T(8,128)S(1)} %convert_multiply_fusion.3), channel_id=1, source_target_pairs={{0,1},{1,2},{2,3},{4,5},{5,6},{6,7},{8,9},{9,10},{10,11},{12,13},{... | collective-permute-start | bytes 393224 | tf_op jit(solution)/shard_map/ppermute | solution.py:17
  15.6 8.7 %collective-permute-start.3 = (f32[8,8,512]{2,1,0:T(8,128)S(1)}, f32[8,8,512]{2,1,0:T(8,128)S(1)}, u32[]{:S(2)}, u32[]{:S(2)}) collective-permute-start(f32[8,8,512]{2,1,0:T(8,128)S(1)} %copy-done.1), channel_id=1, source_target_pairs={{1,0},{2,1},{3,2},{5,4},{6,5},{7,6},{9,8},{10,9},{11,10},{13,12},{... | collective-permute-start | bytes 393224 | tf_op jit(solution)/shard_map/ppermute | solution.py:18
  16.9 7.3 %collective-permute-start.2 = (f32[8,8,512]{2,1,0:T(8,128)S(1)}, f32[8,8,512]{2,1,0:T(8,128)S(1)}, u32[]{:S(2)}, u32[]{:S(2)}) collective-permute-start(f32[8,8,512]{2,1,0:T(8,128)S(1)} %copy-done.1), channel_id=1, source_target_pairs={{0,1},{1,2},{2,3},{4,5},{5,6},{6,7},{8,9},{9,10},{10,11},{12,13},{... | collective-permute-start | bytes 393224 | tf_op jit(solution)/shard_map/ppermute | solution.py:17
  21.8 0.7 copy-start.6
  21.8 7.1 %copy-start.13 = (pred[10]{0:T(512)(128)(4,1)}, pred[10]{0:T(512)(128)(4,1)S(1)}, u32[]{:S(2)}) copy-start(pred[10]{0:T(512)(128)(4,1)S(1)} %compare_and_fusion.6) | copy-start | bytes 34
  21.8 6.6 %copy-start.15 = (pred[12]{0:T(512)(128)(4,1)}, pred[12]{0:T(512)(128)(4,1)S(1)}, u32[]{:S(2)}) copy-start(pred[12]{0:T(512)(128)(4,1)S(1)} %compare_and_fusion.5) | copy-start | bytes 40
  21.9 6.2 %copy-start.17 = (pred[14]{0:T(512)(128)(4,1)}, pred[14]{0:T(512)(128)(4,1)S(1)}, u32[]{:S(2)}) copy-start(pred[14]{0:T(512)(128)(4,1)S(1)} %compare_and_fusion.4) | copy-start | bytes 46
  21.9 5.7 %copy-start.19 = (pred[16]{0:T(512)(128)(4,1)}, pred[16]{0:T(512)(128)(4,1)S(1)}, u32[]{:S(2)}) copy-start(pred[16]{0:T(512)(128)(4,1)S(1)} %compare_and_fusion.3) | copy-start | bytes 52
  21.9 5.0 %copy-start.7 = (pred[18]{0:T(512)(128)(4,1)}, pred[18]{0:T(512)(128)(4,1)S(1)}, u32[]{:S(2)}) copy-start(pred[18]{0:T(512)(128)(4,1)S(1)} %compare_and_fusion.2) | copy-start | bytes 58
  22.5 3.8 %copy-start.9 = (pred[20]{0:T(512)(128)(4,1)}, pred[20]{0:T(512)(128)(4,1)S(1)}, u32[]{:S(2)}) copy-start(pred[20]{0:T(512)(128)(4,1)S(1)} %compare_and_fusion.1) | copy-start | bytes 64
  22.5 0.7 copy-start.21
  23.3 0.7 copy-start.22
  23.9 1.8 copy-start.11
  29.3 0.8 copy-start.3
  31.0 158.2 %all-reduce.30.cloned.1.call-start = ((), (), s32[]{:S(2)}) async-start(), calls=%async_computation.1 | async-start | bytes 262144 | tf_op jit(solution)/shard_map/psum | solution.py:64
  42.6 47.1 %copy-start = (f32[8,8,512]{2,1,0:T(8,128)S(1)}, f32[8,8,512]{2,1,0:T(8,128)}, u32[]{:S(2)}) copy-start(f32[8,8,512]{2,1,0:T(8,128)} %param.5) | copy-start | bytes 393220
  115.5 6.9 %collective-permute-start.5 = (f32[8,8,512]{2,1,0:T(8,128)S(1)}, f32[8,8,512]{2,1,0:T(8,128)S(1)}, u32[]{:S(2)}, u32[]{:S(2)}) collective-permute-start(f32[8,8,512]{2,1,0:T(8,128)S(1)} %convert_multiply_fusion.1), channel_id=1, source_target_pairs={{1,0},{2,1},{3,2},{5,4},{6,5},{7,6},{9,8},{10,9},{11,10},{13,12},{... | collective-permute-start | bytes 393224 | tf_op jit(solution)/shard_map/ppermute | solution.py:18
  116.8 7.1 %collective-permute-start.4 = (f32[8,8,512]{2,1,0:T(8,128)S(1)}, f32[8,8,512]{2,1,0:T(8,128)S(1)}, u32[]{:S(2)}, u32[]{:S(2)}) collective-permute-start(f32[8,8,512]{2,1,0:T(8,128)S(1)} %convert_multiply_fusion.1), channel_id=1, source_target_pairs={{0,1},{1,2},{2,3},{4,5},{5,6},{6,7},{8,9},{9,10},{10,11},{12,13},{... | collective-permute-start | bytes 393224 | tf_op jit(solution)/shard_map/ppermute | solution.py:17
  123.9 0.6 copy-start.12
  125.1 0.6 copy-start.10
  126.3 0.6 copy-start.8
  127.4 0.7 copy-start.20
  128.5 0.6 copy-start.18
  129.4 0.6 copy-start.16
  130.4 0.7 copy-start.14
  131.5 0.9 copy-start.2
  131.5 0.9 copy-start.4
  189.3 13.5 %copy-start.5 = (f32[8,8,512]{2,1,0:T(8,128)S(1)}, f32[8,8,512]{2,1,0:T(8,128)}, u32[]{:S(2)}) copy-start(f32[8,8,512]{2,1,0:T(8,128)} %all-reduce.30.cloned.1.call-done) | copy-start | bytes 393220
Sparse Core Ops, SparseCore 0:
  31.2 58.4 all-reduce.27
  133.4 55.8 all-reduce.29
where the time goes:
time: 211 us; the launch traced here: 210 us
  waiting for transfers between devices  106 us (50%)
  blocking collectives  29.6 us (14%)
  other arithmetic  28.2 us (13%)
  starting transfers between devices  19.5 us (9%)
  between operations  18.8 us (9%)
  local copies, waits for them, and re-layouts  8.45 us (4%)
    psum x2, waiting for transfers between devices, local(): operate_total = lax.psum(total, 'mem')  103 us
    psum x3, blocking collectives, inner(): return lax.psum(jnp.sum(first * second), 'tile')  29.6 us
    ppermute x3, starting transfers between devices, padded(): before = lax.ppermute(last, axis, up)  15.5 us
    unnamed x4, other arithmetic  11.7 us
    unnamed x47, local copies, waits for them, and re-layouts  7.61 us
    select_n x14, other arithmetic, local(): extended = jnp.where(inside[None, :, None], extended, 0.0)  6.44 us
    reduce_sum x3, other arithmetic, inner(): return lax.psum(jnp.sum(first * second), 'tile')  4.72 us
  transfers between devices with their start and end apart: 8, of which 5 were waited for; matrix products, arithmetic and copies ran while one was open for 6% of the time, Pallas kernels for 0%

commit v1 on v0

--- a/solution.py
+++ b/solution.py
@@ -1,10 +1,340 @@
+import functools
+
 import jax
 import jax.numpy as jnp
 from jax import lax
+from jax.experimental import pallas as pl
+from jax.experimental.pallas import tpu as pltpu
 from jax.sharding import PartitionSpec as P
 
 SWEEPS = 8
 ITERS = 2
+MESH = pl.DeviceIdType.MESH
+
+
+def lanes_sum(x):
+    total = x[:, 0:128]
+    for j in range(1, x.shape[1] // 128):
+        total = total + x[:, j * 128 : (j + 1) * 128]
+    return jnp.sum(total, axis=0, keepdims=True)
+
+
+def kernel(M, T, r0_ref, pert_ref, kap_ref, idx_ref, prec_ref, inc_ref, res_ref,
+           pf, gat, halo_k, halo_r, halo_q, xt, cb, fld, tot, ext, q0a, q1a, st, sm,
+           a_s, a_r, f_s, f_r, h_s, h_r, q_s, q_r, g_s, g_r, t_s, t_r, m_s, m_r):
+    m = lax.axis_index("mem")
+    t = lax.axis_index("tile")
+    has_up = t > 0
+    has_dn = t < T - 1
+    levels, R, W = r0_ref.shape
+    E = 3 * R
+    sends = []
+
+    def rc(src, dst, ss, rs, **dev):
+        return pltpu.make_async_remote_copy(
+            src_ref=src, dst_ref=dst, send_sem=ss, recv_sem=rs, device_id=dev, device_id_type=MESH)
+
+    def rows_of(j):
+        return pl.ds(pl.multiple_of(j * R, R), R)
+
+    def mem_at(k):
+        return lax.rem(m + k, M)
+
+    def mem_from(k):
+        return lax.rem(m + M - k, M)
+
+    barrier = pltpu.get_barrier_semaphore()
+    for k in range(1, M):
+        pl.semaphore_signal(barrier, inc=1, device_id={"mem": mem_at(k)}, device_id_type=MESH)
+    for k in range(1, T):
+        pl.semaphore_signal(barrier, inc=1, device_id={"tile": lax.rem(t + k, T)}, device_id_type=MESH)
+    pf[...] = pert_ref[0].astype(jnp.float32)
+    pl.semaphore_wait(barrier, M + T - 2)
+
+    def a2a(k):
+        return rc(pf.at[mem_at(k)], gat.at[1, rows_of(m)], a_s.at[k], a_r.at[k], mem=mem_at(k))
+
+    def a2a_in(k):
+        return rc(pf.at[mem_at(k)], gat.at[1, rows_of(mem_from(k))], a_s.at[k], a_r.at[k], mem=mem_at(k))
+
+    def pair(src, buf, s_sem, r_sem, base):
+        up = rc(src, buf.at[1], s_sem.at[base], r_sem.at[base], tile=t - 1)
+        dn = rc(src, buf.at[0], s_sem.at[base + 1], r_sem.at[base + 1], tile=t + 1)
+        return up, dn
+
+    def start_pair(p):
+        @pl.when(has_up)
+        def _():
+            p[0].start()
+
+        @pl.when(has_dn)
+        def _():
+            p[1].start()
+
+    def recv_pair(p):
+        @pl.when(has_dn)
+        def _():
+            p[0].wait_recv()
+
+        @pl.when(has_up)
+        def _():
+            p[1].wait_recv()
+
+    def send_pair(p):
+        @pl.when(has_up)
+        def _():
+            p[0].wait_send()
+
+        @pl.when(has_dn)
+        def _():
+            p[1].wait_send()
+
+    def fwd(k):
+        j = mem_from(k)
+        src = pf.at[m] if k == 0 else gat.at[1, rows_of(j)]
+        up = rc(src, gat.at[2, rows_of(j)], f_s.at[k], f_r.at[k], tile=t - 1)
+        dn = rc(src, gat.at[0, rows_of(j)], f_s.at[M + k], f_r.at[M + k], tile=t + 1)
+        return up, dn
+
+    for k in range(1, M):
+        a2a(k).start()
+    start_pair(fwd(0))
+    kp = pair(kap_ref.at[m], halo_k, h_s, h_r, 0)
+    rp = pair(r0_ref.at[m], halo_r, h_s, h_r, 2)
+    start_pair(kp)
+    start_pair(rp)
+    gat[1, rows_of(m), :] = pf[m]
+
+    @pl.when(jnp.logical_not(has_up))
+    def _():
+        gat[0] = jnp.zeros_like(gat[0])
+        halo_k[0] = jnp.zeros_like(halo_k[0])
+        halo_r[0] = jnp.zeros_like(halo_r[0])
+        halo_q[0] = jnp.zeros_like(halo_q[0])
+
+    @pl.when(jnp.logical_not(has_dn))
+    def _():
+        gat[2] = jnp.zeros_like(gat[2])
+        halo_k[1] = jnp.zeros_like(halo_k[1])
+        halo_r[1] = jnp.zeros_like(halo_r[1])
+        halo_q[1] = jnp.zeros_like(halo_q[1])
+
+    nobs = idx_ref.shape[1]
+    step_obs = 256 if nobs % 256 == 0 else nobs
+    weight = jnp.zeros((R, W), jnp.float32)
+    for c in range(nobs // step_obs):
+        idx = idx_ref[:, c * step_obs : (c + 1) * step_obs]
+        prec = prec_ref[:, c * step_obs : (c + 1) * step_obs]
+        line = idx // W - m * R
+        col = idx % W
+        hit = lax.broadcasted_iota(jnp.int32, (R, step_obs), 0) == line
+        left = jnp.where(hit, prec, 0.0)
+        first = left.astype(jnp.bfloat16)
+        rest = left - first.astype(jnp.float32)
+        second = rest.astype(jnp.bfloat16)
+        third = (rest - second.astype(jnp.float32)).astype(jnp.bfloat16)
+        hot = (lax.broadcasted_iota(jnp.int32, (W, step_obs), 0) == col)
+        hot = jnp.where(hot, 1.0, 0.0).astype(jnp.bfloat16)
+        for piece in (first, second, third):
+            weight = weight + lax.dot_general(
+                piece, hot, (((1,), (1,)), ((), ())), preferred_element_type=jnp.float32)
+
+    for k in range(1, M):
+        a2a_in(k).wait_recv()
+        start_pair(fwd(k))
+
+    recv_pair(kp)
+    recv_pair(rp)
+    kx = jnp.concatenate([halo_k[0], kap_ref[m], halo_k[1]], axis=0)
+    lane = lax.broadcasted_iota(jnp.int32, (E, W), 1)
+    line = lax.broadcasted_iota(jnp.int32, (E, W), 0)
+    inside = (line + (t - 1) * R >= 0) & (line + (t - 1) * R < T * R)
+    east = jnp.where(lane == W - 1, 0.0, pltpu.roll(kx, W - 1, axis=1))
+    west = jnp.where(lane == 0, 0.0, pltpu.roll(kx, 1, axis=1))
+    north = pltpu.roll(kx, 1, axis=0)
+    south = pltpu.roll(kx, E - 1, axis=0)
+    ce = 0.5 * (kx + east)
+    cw = 0.5 * (kx + west)
+    cn = 0.5 * (kx + north)
+    cs = 0.5 * (kx + south)
+    ca = 1.0 - ((ce + cw) + (cn + cs))
+    ce = jnp.where(lane == W - 1, 0.0, ce)
+    cw = jnp.where(lane == 0, 0.0, cw)
+    for i, c in enumerate((ca, ce, cw, cn, cs)):
+        c = jnp.where(inside, c, 0.0)
+        for e in range(1, E - 1):
+            cb[i, e] = jnp.broadcast_to(c[e : e + 1], (M, W))
+
+    for k in range(M):
+        recv_pair(fwd(k))
+
+    def localize(first):
+        if first:
+            for part in range(3):
+                for j in range(W // 128):
+                    cols = slice(j * 128, (j + 1) * 128)
+                    block = gat[part, :, cols].reshape(M, R, 128)
+                    xt[part * R : (part + 1) * R, :, cols] = jnp.swapaxes(block, 0, 1)
+        for e in range(E):
+            xe = xt[e]
+            fld[0, e] = xe * jnp.broadcast_to(ext[e : e + 1, :], (M, W))
+        for s in range(SWEEPS):
+            a, b = s % 2, (s + 1) % 2
+            count = E - 2 - 2 * s
+
+            def one(i, carry, a=a, b=b, s=s):
+                for u in range(2):
+                    e = s + 1 + 2 * i + u
+                    v = fld[a, e]
+                    out = cb[0, e] * v
+                    out = out + cb[1, e] * pltpu.roll(v, W - 1, axis=1)
+                    out = out + cb[2, e] * pltpu.roll(v, 1, axis=1)
+                    out = out + cb[3, e] * fld[a, e - 1]
+                    out = out + cb[4, e] * fld[a, e + 1]
+                    fld[b, e] = out
+                return carry
+
+            lax.fori_loop(0, count // 2, one, 0)
+        z = SWEEPS % 2
+        for r in range(R):
+            tot[r : r + 1, :] = jnp.sum(xt[R + r] * fld[z, R + r], axis=0, keepdims=True)
+        return tot[...]
+
+    def gather(buf, base):
+        out = []
+        for k in range(1, M):
+            out.append(rc(buf.at[m], buf.at[m], g_s.at[base + k], g_r.at[base + k], mem=mem_at(k)))
+        return out
+
+    def gather_in(buf, base):
+        for k in range(1, M):
+            j = mem_from(k)
+            rc(buf.at[j], buf.at[j], g_s.at[base + k], g_r.at[base + k], mem=mem_at(k)).wait_recv()
+
+    def tile_sum_start(n, vals):
+        zero = jnp.zeros((8 - len(vals), 128), jnp.float32)
+        st[n, t] = jnp.concatenate(list(vals) + [zero], axis=0)
+        for k in range(1, T):
+            c = rc(st.at[n, t], st.at[n, t], t_s.at[n * T + k], t_r.at[n * T + k], tile=lax.rem(t + k, T))
+            c.start()
+            sends.append(c)
+
+    def mem_sum_start(n):
+        for k in range(1, T):
+            j = lax.rem(t + T - k, T)
+            rc(st.at[n, j], st.at[n, j], t_s.at[n * T + k], t_r.at[n * T + k], tile=lax.rem(t + k, T)).wait_recv()
+        total = st[n, 0]
+        for j in range(1, T):
+            total = total + st[n, j]
+        sm[n, m] = total
+        for k in range(1, M):
+            c = rc(sm.at[n, m], sm.at[n, m], m_s.at[n * M + k], m_r.at[n * M + k], mem=mem_at(k))
+            c.start()
+            sends.append(c)
+
+    def mem_sum_end(n):
+        for k in range(1, M):
+            j = mem_from(k)
+            rc(sm.at[n, j], sm.at[n, j], m_s.at[n * M + k], m_r.at[n * M + k], mem=mem_at(k)).wait_recv()
+        total = sm[n, 0]
+        for j in range(1, M):
+            total = total + sm[n, j]
+        return jnp.sum(total, axis=1, keepdims=True)
+
+    inv = 1.0 / M
+    r0 = r0_ref[m]
+    ext[0:R] = halo_r[0]
+    ext[R : 2 * R] = r0
+    ext[2 * R : E] = halo_r[1]
+    q0 = r0 + weight * r0 + localize(True) * inv
+    q0a[m] = q0
+    qp = pair(q0a.at[m], halo_q, q_s, q_r, 0)
+    start_pair(qp)
+    tile_sum_start(0, (lanes_sum(r0 * r0), lanes_sum(r0 * q0)))
+    g0 = gather(q0a, 0)
+    for c in g0:
+        c.start()
+    recv_pair(qp)
+    mem_sum_start(0)
+    ext[0:R] = halo_q[0]
+    ext[R : 2 * R] = q0
+    ext[2 * R : E] = halo_q[1]
+    q1 = q0 + weight * q0 + localize(False) * inv
+    q1a[m] = q1
+    g1 = gather(q1a, M)
+    for c in g1:
+        c.start()
+    dots = mem_sum_end(0)
+    rr, rq = dots[0:1], dots[1:2]
+    alpha = rr / rq
+    r1 = r0 - alpha * q0
+    ar1 = q0 - alpha * q1
+    tile_sum_start(1, (lanes_sum(r1 * r1), lanes_sum(r1 * ar1), lanes_sum(r1 * q0)))
+    mem_sum_start(1)
+    gather_in(q0a, 0)
+    gather_in(q1a, M)
+    dots = mem_sum_end(1)
+    new = dots[0:1]
+    beta = new / rr
+    den = dots[1:2] + 2.0 * beta * dots[2:3] + beta * beta * rq
+    alpha2 = new / den
+    for l in range(levels):
+        b = r0_ref[l]
+        q = q0a[l]
+        r1 = b - alpha * q
+        inc_ref[l] = alpha * b + alpha2 * (r1 + beta * b)
+        res_ref[l] = r1 - alpha2 * ((q - alpha * q1a[l]) + beta * q)
+
+    for k in range(1, M):
+        a2a(k).wait_send()
+    for k in range(M):
+        send_pair(fwd(k))
+    send_pair(kp)
+    send_pair(rp)
+    send_pair(qp)
+    for c in g0 + g1 + sends:
+        c.wait_send()
+
+
+def fused(M, T, right_side, members, diffusivity, obs_index, obs_precision):
+    levels, R, W = right_side.shape
+    f32 = jnp.float32
+    dma = pltpu.SemaphoreType.DMA
+    vmem = pl.BlockSpec(memory_space=pltpu.VMEM)
+    out = jax.ShapeDtypeStruct(right_side.shape, f32)
+    E = 3 * R
+    return pl.pallas_call(
+        functools.partial(kernel, M, T),
+        name="cg",
+        out_shape=(out, out),
+        in_specs=[vmem] * 5,
+        out_specs=(vmem, vmem),
+        scratch_shapes=[
+            pltpu.VMEM((levels, R, W), f32),
+            pltpu.VMEM((3, M * R, W), f32),
+            pltpu.VMEM((2, R, W), f32),
+            pltpu.VMEM((2, R, W), f32),
+            pltpu.VMEM((2, R, W), f32),
+            pltpu.VMEM((E, M, W), f32),
+            pltpu.VMEM((5, E, M, W), f32),
+            pltpu.VMEM((2, E, M, W), f32),
+            pltpu.VMEM((R, W), f32),
+            pltpu.VMEM((E, W), f32),
+            pltpu.VMEM((levels, R, W), f32),
+            pltpu.VMEM((levels, R, W), f32),
+            pltpu.VMEM((2, T, 8, 128), f32),
+            pltpu.VMEM((2, M, 8, 128), f32),
+            dma((M,)), dma((M,)),
+            dma((2 * M,)), dma((2 * M,)),
+            dma((4,)), dma((4,)),
+            dma((2,)), dma((2,)),
+            dma((2 * M,)), dma((2 * M,)),
+            dma((2 * T,)), dma((2 * T,)),
+            dma((2 * M,)), dma((2 * M,)),
+        ],
+        compiler_params=pltpu.CompilerParams(
+            collective_id=0, has_side_effects=True, vmem_limit_bytes=40 * 1024 * 1024),
+    )(right_side, members, diffusivity, obs_index.reshape(1, -1), obs_precision.reshape(1, -1))
 
 
 def padded(shard, sides, width):
@@ -32,7 +362,7 @@
     return centre + flux
 
 
-def local(right_side, members, diffusivity, obs_index, obs_precision):
+def general(right_side, members, diffusivity, obs_index, obs_precision):
     levels, rows, width = right_side.shape
     level = obs_index // (rows * width)
     row_pos = obs_index // width % rows
@@ -82,4 +412,13 @@
         P("tile"),
     )
     out_specs = (P(None, "tile", None), P(None, "tile", None))
+    M, T = mesh.shape["mem"], mesh.shape["tile"]
+
+    def local(right_side, members, diffusivity, obs_index, obs_precision):
+        levels, rows, width = right_side.shape
+        fits = levels == M and members.shape[0] == 1 and rows == SWEEPS and M == 8
+        if fits and ITERS == 2 and width % 128 == 0:
+            return fused(M, T, right_side, members, diffusivity, obs_index, obs_precision)
+        return general(right_side, members, diffusivity, obs_index, obs_precision)
+
     return jax.shard_map(local, mesh=mesh, in_specs=in_specs, out_specs=out_specs, check_vma=False)

time: 211 us -> 42.9 us (0.20)
  waiting for transfers between devices: 106 us -> 0 us
  Pallas kernels: 0 us -> 36.7 us
  blocking collectives: 29.6 us -> 0 us
  other arithmetic: 28.2 us -> 0 us
  starting transfers between devices: 19.5 us -> 0 us
  between operations: 18.8 us -> 0.65 us
  local copies, waits for them, and re-layouts: 8.45 us -> 5.35 us
    psum x2 -> x0, waiting for transfers between devices: 103 us -> none  [local(): operate_total = lax.psum(total, 'mem')]
    pallas_call x0 -> x1, Pallas kernels: none -> 36.7 us  [fused(): pl.pallas_call(functools.partial(kernel, M, T), name='cg', out_shape=(out...]
    psum x3 -> x0, blocking collectives: 29.6 us -> none  [inner(): return lax.psum(jnp.sum(first * second), 'tile')]
    ppermute x6 -> x0, starting transfers between devices: 19.4 us -> none  [the longest x3 15.5 us: padded(): before = lax.ppermute(last, axis, up)]
    unnamed x4 -> x0, other arithmetic: 11.7 us -> none
    select_n x15 -> x0, other arithmetic: 6.47 us -> none  [the longest x14 6.44 us: local(): extended = jnp.where(inside[None, :, None], extended, 0.0)]
    reduce_sum x3 -> x0, other arithmetic: 4.72 us -> none  [inner(): return lax.psum(jnp.sum(first * second), 'tile')]
    mul x4 -> x0, other arithmetic: 3.55 us -> none  [the longest x2 1.82 us: local(): extended = padded(pert * direction, (('tile', 1),), SWEEPS)]
  transfers between devices with their start and end apart: 8 -> 0, of which waited for: 5 -> 0; matrix products, arithmetic and copies ran while one was open for 6% -> 0% of each run, Pallas kernels for 0% -> 0%
where the time goes in v1:
time: 42.9 us; the launch traced here: 42.7 us
  Pallas kernels  36.7 us (86%)
  local copies, waits for them, and re-layouts  5.35 us (12%)
  between operations  0.65 us (2%)
    pallas_call x1, Pallas kernels, fused(): pl.pallas_call(functools.partial(kernel, M, T), name='cg', out_shape=(out...  36.7 us
    unnamed x12, local copies, waits for them, and re-layouts  5.35 us

profile of v1, /device:TPU:0, one launch (start us, length us, event | category | flops | bytes accessed | tf_op | source)
XLA Modules:
  0.0 42.7 jit_solution(12617103128279902843)
XLA Ops:
  0.6 0.0 copy-start
  0.6 0.9 %copy-done = f32[8,8,512]{2,1,0:T(8,128)S(1)} copy-done((f32[8,8,512]{2,1,0:T(8,128)S(1)}, f32[8,8,512]{2,1,0:T(8,128)}, u32[]{:S(2)}) %copy-start) | copy-done | bytes 131096
  1.5 0.0 copy-start.1
  1.5 0.9 %copy-done.1 = f32[8,8,512]{2,1,0:T(8,128)S(1)} copy-done((f32[8,8,512]{2,1,0:T(8,128)S(1)}, f32[8,8,512]{2,1,0:T(8,128)}, u32[]{:S(2)}) %copy-start.1) | copy-done | bytes 131096
  2.4 0.0 copy-start.2
  2.4 0.8 %copy-done.2 = bf16[1,8,8,512]{3,2,1,0:T(8,128)(2,1)S(1)} copy-done((bf16[1,8,8,512]{3,2,1,0:T(8,128)(2,1)S(1)}, bf16[1,8,8,512]{3,2,1,0:T(8,128)(2,1)}, u32[]{:S(2)}) %copy-start.2) | copy-done | bytes 65560
  3.3 0.0 copy-start.3
  3.3 0.7 %copy-done.3 = s32[2048]{0:T(1024)S(1)} copy-done((s32[2048]{0:T(1024)S(1)}, s32[2048]{0:T(1024)}, u32[]{:S(2)}) %copy-start.3) | copy-done | bytes 8216
  4.0 0.0 copy-start.4
  4.0 0.7 %copy-done.4 = f32[2048]{0:T(1024)S(1)} copy-done((f32[2048]{0:T(1024)S(1)}, f32[2048]{0:T(1024)}, u32[]{:S(2)}) %copy-start.4) | copy-done | bytes 8216
  4.7 36.7 %cg.1 = (f32[8,8,512]{2,1,0:T(8,128)S(1)}, f32[8,8,512]{2,1,0:T(8,128)S(1)}) custom-call(f32[8,8,512]{2,1,0:T(8,128)S(1)} %copy-done, bf16[1,8,8,512]{3,2,1,0:T(8,128)(2,1)S(1)} %copy-done.2, f32[8,8,512]{2,1,0:T(8,128)S(1)} %copy-done.1, s32[1,2048]{1,0:T(1,128)S(1)} %bitcast.2, f32[1,2048]{1,0:T(1,128)S(1)} %bitcast.3), custom_call_target="tpu_custom_call" | custom-call | tf_op jit(solution)/shard_map/cg/pallas_call | solution.py:306
  41.4 0.7 %copy.9 = f32[8,8,512]{2,1,0:T(8,128)} copy(f32[8,8,512]{2,1,0:T(8,128)S(1)} %get-tuple-element.4) | data formatting | bytes 262144
  42.0 0.7 %copy.10 = f32[8,8,512]{2,1,0:T(8,128)} copy(f32[8,8,512]{2,1,0:T(8,128)S(1)} %get-tuple-element.5) | data formatting | bytes 262144
Async XLA Ops:
  0.6 0.9 %copy-start = (f32[8,8,512]{2,1,0:T(8,128)S(1)}, f32[8,8,512]{2,1,0:T(8,128)}, u32[]{:S(2)}) copy-start(f32[8,8,512]{2,1,0:T(8,128)} %r0_ref.1) | copy-start | bytes 393220
  1.5 0.9 %copy-start.1 = (f32[8,8,512]{2,1,0:T(8,128)S(1)}, f32[8,8,512]{2,1,0:T(8,128)}, u32[]{:S(2)}) copy-start(f32[8,8,512]{2,1,0:T(8,128)} %kap_ref.1) | copy-start | bytes 393220
  2.4 0.8 %copy-start.2 = (bf16[1,8,8,512]{3,2,1,0:T(8,128)(2,1)S(1)}, bf16[1,8,8,512]{3,2,1,0:T(8,128)(2,1)}, u32[]{:S(2)}) copy-start(bf16[1,8,8,512]{3,2,1,0:T(8,128)(2,1)} %pert_ref.1) | copy-start | bytes 196612
  3.3 0.7 %copy-start.3 = (s32[2048]{0:T(1024)S(1)}, s32[2048]{0:T(1024)}, u32[]{:S(2)}) copy-start(s32[2048]{0:T(1024)} %param.8) | copy-start | bytes 24580
  4.0 0.7 %copy-start.4 = (f32[2048]{0:T(1024)S(1)}, f32[2048]{0:T(1024)}, u32[]{:S(2)}) copy-start(f32[2048]{0:T(1024)} %param.9) | copy-start | bytes 24580

commit v2 on v1

--- a/solution.py
+++ b/solution.py
@@ -19,8 +19,8 @@
     return jnp.sum(total, axis=0, keepdims=True)
 
 
-def kernel(M, T, r0_ref, pert_ref, kap_ref, idx_ref, prec_ref, inc_ref, res_ref,
-           pf, gat, halo_k, halo_r, halo_q, xt, cb, fld, tot, ext, q0a, q1a, st, sm,
+def kernel(M, T, r0_hbm, pert_hbm, kap_hbm, idx_hbm, prec_hbm, inc_ref, res_ref,
+           r0_ref, pert_ref, kap_ref, idx_ref, prec_ref, l_s, pf, gat, halo_k, halo_r, halo_q, xt, cb, fld, tot, ext, q0a, q1a, st, sm,
            a_s, a_r, f_s, f_r, h_s, h_r, q_s, q_r, g_s, g_r, t_s, t_r, m_s, m_r):
     m = lax.axis_index("mem")
     t = lax.axis_index("tile")
@@ -43,12 +43,23 @@
     def mem_from(k):
         return lax.rem(m + M - k, M)
 
+    loads = [
+        pltpu.make_async_copy(pert_hbm.at[0], pert_ref, l_s.at[0]),
+        pltpu.make_async_copy(kap_hbm.at[m], kap_ref, l_s.at[1]),
+        pltpu.make_async_copy(r0_hbm, r0_ref, l_s.at[2]),
+        pltpu.make_async_copy(idx_hbm, idx_ref, l_s.at[3]),
+        pltpu.make_async_copy(prec_hbm, prec_ref, l_s.at[4]),
+    ]
+    for c in loads:
+        c.start()
+
     barrier = pltpu.get_barrier_semaphore()
     for k in range(1, M):
         pl.semaphore_signal(barrier, inc=1, device_id={"mem": mem_at(k)}, device_id_type=MESH)
     for k in range(1, T):
         pl.semaphore_signal(barrier, inc=1, device_id={"tile": lax.rem(t + k, T)}, device_id_type=MESH)
-    pf[...] = pert_ref[0].astype(jnp.float32)
+    loads[0].wait()
+    pf[...] = pert_ref[...].astype(jnp.float32)
     pl.semaphore_wait(barrier, M + T - 2)
 
     def a2a(k):
@@ -99,7 +110,9 @@
     for k in range(1, M):
         a2a(k).start()
     start_pair(fwd(0))
-    kp = pair(kap_ref.at[m], halo_k, h_s, h_r, 0)
+    loads[1].wait()
+    loads[2].wait()
+    kp = pair(kap_ref, halo_k, h_s, h_r, 0)
     rp = pair(r0_ref.at[m], halo_r, h_s, h_r, 2)
     start_pair(kp)
     start_pair(rp)
@@ -119,6 +132,8 @@
         halo_r[1] = jnp.zeros_like(halo_r[1])
         halo_q[1] = jnp.zeros_like(halo_q[1])
 
+    loads[3].wait()
+    loads[4].wait()
     nobs = idx_ref.shape[1]
     step_obs = 256 if nobs % 256 == 0 else nobs
     weight = jnp.zeros((R, W), jnp.float32)
@@ -145,7 +160,7 @@
 
     recv_pair(kp)
     recv_pair(rp)
-    kx = jnp.concatenate([halo_k[0], kap_ref[m], halo_k[1]], axis=0)
+    kx = jnp.concatenate([halo_k[0], kap_ref[...], halo_k[1]], axis=0)
     lane = lax.broadcasted_iota(jnp.int32, (E, W), 1)
     line = lax.broadcasted_iota(jnp.int32, (E, W), 0)
     inside = (line + (t - 1) * R >= 0) & (line + (t - 1) * R < T * R)
@@ -165,36 +180,34 @@
         for e in range(1, E - 1):
             cb[i, e] = jnp.broadcast_to(c[e : e + 1], (M, W))
 
+    def turn(part):
+        for j in range(W // 128):
+            cols = slice(j * 128, (j + 1) * 128)
+            block = gat[part, :, cols].reshape(M, R, 128)
+            xt[part * R : (part + 1) * R, :, cols] = jnp.swapaxes(block, 0, 1)
+
+    turn(1)
     for k in range(M):
         recv_pair(fwd(k))
-
-    def localize(first):
-        if first:
-            for part in range(3):
-                for j in range(W // 128):
-                    cols = slice(j * 128, (j + 1) * 128)
-                    block = gat[part, :, cols].reshape(M, R, 128)
-                    xt[part * R : (part + 1) * R, :, cols] = jnp.swapaxes(block, 0, 1)
+    turn(0)
+    turn(2)
+
+    def localize():
         for e in range(E):
             xe = xt[e]
             fld[0, e] = xe * jnp.broadcast_to(ext[e : e + 1, :], (M, W))
         for s in range(SWEEPS):
             a, b = s % 2, (s + 1) % 2
-            count = E - 2 - 2 * s
-
-            def one(i, carry, a=a, b=b, s=s):
-                for u in range(2):
-                    e = s + 1 + 2 * i + u
-                    v = fld[a, e]
-                    out = cb[0, e] * v
-                    out = out + cb[1, e] * pltpu.roll(v, W - 1, axis=1)
-                    out = out + cb[2, e] * pltpu.roll(v, 1, axis=1)
-                    out = out + cb[3, e] * fld[a, e - 1]
-                    out = out + cb[4, e] * fld[a, e + 1]
-                    fld[b, e] = out
-                return carry
-
-            lax.fori_loop(0, count // 2, one, 0)
+            above, here = fld[a, s], fld[a, s + 1]
+            for e in range(s + 1, E - 1 - s):
+                below = fld[a, e + 1]
+                out = cb[0, e] * here
+                out = out + cb[3, e] * above
+                out = out + cb[4, e] * below
+                out = out + cb[1, e] * pltpu.roll(here, W - 1, axis=1)
+                out = out + cb[2, e] * pltpu.roll(here, 1, axis=1)
+                fld[b, e] = out
+                above, here = here, below
         z = SWEEPS % 2
         for r in range(R):
             tot[r : r + 1, :] = jnp.sum(xt[R + r] * fld[z, R + r], axis=0, keepdims=True)
@@ -246,7 +259,7 @@
     ext[0:R] = halo_r[0]
     ext[R : 2 * R] = r0
     ext[2 * R : E] = halo_r[1]
-    q0 = r0 + weight * r0 + localize(True) * inv
+    q0 = r0 + weight * r0 + localize() * inv
     q0a[m] = q0
     qp = pair(q0a.at[m], halo_q, q_s, q_r, 0)
     start_pair(qp)
@@ -259,7 +272,7 @@
     ext[0:R] = halo_q[0]
     ext[R : 2 * R] = q0
     ext[2 * R : E] = halo_q[1]
-    q1 = q0 + weight * q0 + localize(False) * inv
+    q1 = q0 + weight * q0 + localize() * inv
     q1a[m] = q1
     g1 = gather(q1a, M)
     for c in g1:
@@ -307,9 +320,15 @@
         functools.partial(kernel, M, T),
         name="cg",
         out_shape=(out, out),
-        in_specs=[vmem] * 5,
+        in_specs=[pl.BlockSpec(memory_space=pltpu.HBM)] * 5,
         out_specs=(vmem, vmem),
         scratch_shapes=[
+            pltpu.VMEM((levels, R, W), f32),
+            pltpu.VMEM((levels, R, W), members.dtype),
+            pltpu.VMEM((R, W), f32),
+            pltpu.VMEM((1, obs_index.shape[0]), jnp.int32),
+            pltpu.VMEM((1, obs_index.shape[0]), f32),
+            dma((5,)),
             pltpu.VMEM((levels, R, W), f32),
             pltpu.VMEM((3, M * R, W), f32),
             pltpu.VMEM((2, R, W), f32),
@@ -333,7 +352,7 @@
             dma((2 * M,)), dma((2 * M,)),
         ],
         compiler_params=pltpu.CompilerParams(
-            collective_id=0, has_side_effects=True, vmem_limit_bytes=40 * 1024 * 1024),
+            collective_id=0, has_side_effects=True),
     )(right_side, members, diffusivity, obs_index.reshape(1, -1), obs_precision.reshape(1, -1))
 
 

time: 42.9 us -> 35.1 us (0.82)
  Pallas kernels: 36.7 us -> 32 us
  local copies, waits for them, and re-layouts: 5.35 us -> 2.26 us
    pallas_call x1, Pallas kernels: 36.7 us -> 32 us  [fused(): pl.pallas_call(functools.partial(kernel, M, T), name='cg', out_shape=(out...]
    unnamed x12 -> x4, local copies, waits for them, and re-layouts: 5.35 us -> 2.26 us
where the time goes in v2:
time: 35.1 us; the launch traced here: 34.9 us
  Pallas kernels  32 us (91%)
  local copies, waits for them, and re-layouts  2.26 us (6%)
  between operations  0.65 us (2%)
    pallas_call x1, Pallas kernels, fused(): pl.pallas_call(functools.partial(kernel, M, T), name='cg', out_shape=(out...  32 us
    unnamed x4, local copies, waits for them, and re-layouts  2.26 us

profile of v2, /device:TPU:0, one launch (start us, length us, event | category | flops | bytes accessed | tf_op | source)
XLA Modules:
  0.0 34.9 jit_solution(2807255697534439646)
XLA Ops:
  0.6 32.0 %cg.1 = (f32[8,8,512]{2,1,0:T(8,128)}, f32[8,8,512]{2,1,0:T(8,128)}) custom-call(f32[8,8,512]{2,1,0:T(8,128)} %r0_hbm.1, bf16[1,8,8,512]{3,2,1,0:T(8,128)(2,1)} %pert_hbm.1, f32[8,8,512]{2,1,0:T(8,128)} %kap_hbm.1, s32[1,2048]{1,0:T(1,128)} %bitcast.2, f32[1,2048]{1,0:T(1,128)} %bitcast.3), custom_call_target="tpu_custom_call" | custom-call | tf_op jit(solution)/shard_map/cg/pallas_call | solution.py:319
  32.6 0.0 copy-start
  32.6 1.6 %copy.9 = f32[8,8,512]{2,1,0:T(8,128)} copy(f32[8,8,512]{2,1,0:T(8,128)} %get-tuple-element.4) | data formatting | bytes 262144
  34.3 0.0 copy-done
  34.3 0.7 %copy.10 = f32[8,8,512]{2,1,0:T(8,128)} copy(f32[8,8,512]{2,1,0:T(8,128)S(1)} %copy-done) | data formatting | bytes 262144
Async XLA Ops:
  32.6 1.6 %copy-start = (f32[8,8,512]{2,1,0:T(8,128)S(1)}, f32[8,8,512]{2,1,0:T(8,128)}, u32[]{:S(2)}) copy-start(f32[8,8,512]{2,1,0:T(8,128)} %get-tuple-element.5) | copy-start | bytes 393220

commit v3 on v2

--- a/solution.py
+++ b/solution.py
@@ -20,8 +20,8 @@
 
 
 def kernel(M, T, r0_hbm, pert_hbm, kap_hbm, idx_hbm, prec_hbm, inc_ref, res_ref,
-           r0_ref, pert_ref, kap_ref, idx_ref, prec_ref, l_s, pf, gat, halo_k, halo_r, halo_q, xt, cb, fld, tot, ext, q0a, q1a, st, sm,
-           a_s, a_r, f_s, f_r, h_s, h_r, q_s, q_r, g_s, g_r, t_s, t_r, m_s, m_r):
+           r0_ref, pert_ref, kap_ref, idx_ref, prec_ref, l_s, pf, gat, halo_k, halo_r, halo_q, xt, cb, fld, tot, ext, q0a, q1a, st, go,
+           a_s, a_r, f_s, f_r, h_s, h_r, q_s, q_r, g_s, g_r, t_s, t_r):
     m = lax.axis_index("mem")
     t = lax.axis_index("tile")
     has_up = t > 0
@@ -61,6 +61,8 @@
     loads[0].wait()
     pf[...] = pert_ref[...].astype(jnp.float32)
     pl.semaphore_wait(barrier, M + T - 2)
+    for k in range(1, T):
+        pl.semaphore_signal(go, inc=1, device_id={"tile": lax.rem(t + k, T)}, device_id_type=MESH)
 
     def a2a(k):
         return rc(pf.at[mem_at(k)], gat.at[1, rows_of(m)], a_s.at[k], a_r.at[k], mem=mem_at(k))
@@ -224,35 +226,39 @@
             j = mem_from(k)
             rc(buf.at[j], buf.at[j], g_s.at[base + k], g_r.at[base + k], mem=mem_at(k)).wait_recv()
 
-    def tile_sum_start(n, vals):
-        zero = jnp.zeros((8 - len(vals), 128), jnp.float32)
-        st[n, t] = jnp.concatenate(list(vals) + [zero], axis=0)
-        for k in range(1, T):
-            c = rc(st.at[n, t], st.at[n, t], t_s.at[n * T + k], t_r.at[n * T + k], tile=lax.rem(t + k, T))
+    me = t * M + m
+
+    def all_at(k, sign):
+        km, kt = k % M, k // M
+        if sign > 0:
+            return mem_at(km), lax.rem(t + kt, T)
+        return mem_from(km), lax.rem(t + T - kt, T)
+
+    def scal(n, k, slot):
+        to_m, to_t = all_at(k, 1)
+        at = n * M * T + k
+        return rc(st.at[n, slot], st.at[n, slot], t_s.at[at], t_r.at[at], mem=to_m, tile=to_t)
+
+    def sum_start(n, vals):
+        lane1 = lax.broadcasted_iota(jnp.int32, (1, 128), 1)
+        row = jnp.zeros((1, 128), jnp.float32)
+        for i, v in enumerate(vals):
+            row = jnp.where(lane1 == i, jnp.sum(v, axis=1, keepdims=True), row)
+        st[n, me] = row
+        for k in range(M * T - 1, 0, -1):
+            c = scal(n, k, me)
             c.start()
             sends.append(c)
 
-    def mem_sum_start(n):
-        for k in range(1, T):
-            j = lax.rem(t + T - k, T)
-            rc(st.at[n, j], st.at[n, j], t_s.at[n * T + k], t_r.at[n * T + k], tile=lax.rem(t + k, T)).wait_recv()
-        total = st[n, 0]
-        for j in range(1, T):
-            total = total + st[n, j]
-        sm[n, m] = total
-        for k in range(1, M):
-            c = rc(sm.at[n, m], sm.at[n, m], m_s.at[n * M + k], m_r.at[n * M + k], mem=mem_at(k))
-            c.start()
-            sends.append(c)
-
-    def mem_sum_end(n):
-        for k in range(1, M):
-            j = mem_from(k)
-            rc(sm.at[n, j], sm.at[n, j], m_s.at[n * M + k], m_r.at[n * M + k], mem=mem_at(k)).wait_recv()
-        total = sm[n, 0]
-        for j in range(1, M):
-            total = total + sm[n, j]
-        return jnp.sum(total, axis=1, keepdims=True)
+    def sum_end(n):
+        for k in range(1, M * T):
+            j_m, j_t = all_at(k, -1)
+            scal(n, k, j_t * M + j_m).wait_recv()
+        parts = [st[n, j] for j in range(M * T)]
+        while len(parts) > 1:
+            parts = [parts[i] + parts[i + 1] for i in range(0, len(parts) - 1, 2)] + (
+                [parts[-1]] if len(parts) % 2 else [])
+        return parts[0]
 
     inv = 1.0 / M
     r0 = r0_ref[m]
@@ -262,13 +268,13 @@
     q0 = r0 + weight * r0 + localize() * inv
     q0a[m] = q0
     qp = pair(q0a.at[m], halo_q, q_s, q_r, 0)
+    pl.semaphore_wait(go, T - 1)
+    sum_start(0, (lanes_sum(r0 * r0), lanes_sum(r0 * q0)))
     start_pair(qp)
-    tile_sum_start(0, (lanes_sum(r0 * r0), lanes_sum(r0 * q0)))
     g0 = gather(q0a, 0)
     for c in g0:
         c.start()
     recv_pair(qp)
-    mem_sum_start(0)
     ext[0:R] = halo_q[0]
     ext[R : 2 * R] = q0
     ext[2 * R : E] = halo_q[1]
@@ -277,19 +283,18 @@
     g1 = gather(q1a, M)
     for c in g1:
         c.start()
-    dots = mem_sum_end(0)
-    rr, rq = dots[0:1], dots[1:2]
+    dots = sum_end(0)
+    rr, rq = dots[:, 0:1], dots[:, 1:2]
     alpha = rr / rq
     r1 = r0 - alpha * q0
     ar1 = q0 - alpha * q1
-    tile_sum_start(1, (lanes_sum(r1 * r1), lanes_sum(r1 * ar1), lanes_sum(r1 * q0)))
-    mem_sum_start(1)
+    sum_start(1, (lanes_sum(r1 * r1), lanes_sum(r1 * ar1), lanes_sum(r1 * q0)))
     gather_in(q0a, 0)
     gather_in(q1a, M)
-    dots = mem_sum_end(1)
-    new = dots[0:1]
+    dots = sum_end(1)
+    new = dots[:, 0:1]
     beta = new / rr
-    den = dots[1:2] + 2.0 * beta * dots[2:3] + beta * beta * rq
+    den = dots[:, 1:2] + 2.0 * beta * dots[:, 2:3] + beta * beta * rq
     alpha2 = new / den
     for l in range(levels):
         b = r0_ref[l]
@@ -314,8 +319,9 @@
     f32 = jnp.float32
     dma = pltpu.SemaphoreType.DMA
     vmem = pl.BlockSpec(memory_space=pltpu.VMEM)
-    out = jax.ShapeDtypeStruct(right_side.shape, f32)
+    out = pltpu.VMEM(right_side.shape, f32)
     E = 3 * R
+    operands = (right_side, members, diffusivity, obs_index.reshape(1, -1), obs_precision.reshape(1, -1))
     return pl.pallas_call(
         functools.partial(kernel, M, T),
         name="cg",
@@ -341,19 +347,18 @@
             pltpu.VMEM((E, W), f32),
             pltpu.VMEM((levels, R, W), f32),
             pltpu.VMEM((levels, R, W), f32),
-            pltpu.VMEM((2, T, 8, 128), f32),
-            pltpu.VMEM((2, M, 8, 128), f32),
+            pltpu.VMEM((2, M * T, 1, 128), f32),
+            pltpu.SemaphoreType.REGULAR,
             dma((M,)), dma((M,)),
             dma((2 * M,)), dma((2 * M,)),
             dma((4,)), dma((4,)),
             dma((2,)), dma((2,)),
             dma((2 * M,)), dma((2 * M,)),
-            dma((2 * T,)), dma((2 * T,)),
-            dma((2 * M,)), dma((2 * M,)),
+            dma((2 * M * T,)), dma((2 * M * T,)),
         ],
         compiler_params=pltpu.CompilerParams(
             collective_id=0, has_side_effects=True),
-    )(right_side, members, diffusivity, obs_index.reshape(1, -1), obs_precision.reshape(1, -1))
+    )(*[pltpu.with_memory_space_constraint(x, pltpu.HBM) for x in operands])
 
 
 def padded(shard, sides, width):

time: 35.1 us -> 30.2 us (0.86)
  Pallas kernels: 32 us -> 28.1 us
  local copies, waits for them, and re-layouts: 2.26 us -> 1.31 us
    pallas_call x1, Pallas kernels: 32 us -> 28.1 us  [fused(): pl.pallas_call(functools.partial(kernel, M, T), name='cg', out_shape=(out...]
    unnamed x4 -> x2, local copies, waits for them, and re-layouts: 2.26 us -> 1.31 us
where the time goes in v3:
time: 30.2 us; the launch traced here: 30.1 us
  Pallas kernels  28.1 us (93%)
  local copies, waits for them, and re-layouts  1.31 us (4%)
  between operations  0.64 us (2%)
    pallas_call x1, Pallas kernels, fused(): pl.pallas_call(functools.partial(kernel, M, T), name='cg', out_shape=(out...  28.1 us
    unnamed x2, local copies, waits for them, and re-layouts  1.31 us

profile of v3, /device:TPU:0, one launch (start us, length us, event | category | flops | bytes accessed | tf_op | source)
XLA Modules:
  0.0 30.1 jit_solution(4282600463065093853)
XLA Ops:
  0.6 28.1 %cg.1 = (f32[8,8,512]{2,1,0:T(8,128)S(1)}, f32[8,8,512]{2,1,0:T(8,128)S(1)}) custom-call(f32[8,8,512]{2,1,0:T(8,128)} %r0_hbm.1, bf16[1,8,8,512]{3,2,1,0:T(8,128)(2,1)} %pert_hbm.1, f32[8,8,512]{2,1,0:T(8,128)} %kap_hbm.1, s32[1,2048]{1,0:T(1,128)} %bitcast.2, f32[1,2048]{1,0:T(1,128)} %bitcast.3), custom_call_target="tpu_custom_call" | custom-call | tf_op jit(solution)/shard_map/cg/pallas_call | solution.py:325
  28.7 0.7 %copy.9 = f32[8,8,512]{2,1,0:T(8,128)} copy(f32[8,8,512]{2,1,0:T(8,128)S(1)} %get-tuple-element.2) | data formatting | bytes 262144
  29.4 0.7 %copy.10 = f32[8,8,512]{2,1,0:T(8,128)} copy(f32[8,8,512]{2,1,0:T(8,128)S(1)} %get-tuple-element.3) | data formatting | bytes 262144
